TPU v7x, 32 devices: a whole 2x2x4 slice. The times are simulated.
32 devices in a mesh: grp: 2 (over x), chol: 16 (over z, y, core).
Axes of the slice: x: 2, y: 2, z: 4, core: 2. Of those that a mesh axis runs over, the one named last changes fastest.
Arguments:
- walkers: bfloat16 [1024, 64, 256], P(('grp', 'chol')), parts along dimension 0, may hold values from -6 to 6
- fields: bfloat16 [1024, 1024], P(('grp', 'chol')), parts along dimension 0, may hold values from -6 to 6
- chol_vectors: bfloat16 [1024, 256, 256], P(None, 'chol'), may hold values from -0.375 to 0.375
- rotated: bfloat16 [1024, 64, 256], P(None, 'chol'), may hold values from -0.046875 to 0.046875
- send_walker: int32 [32, 16, 2], P(('grp', 'chol')), parts along dimension 0, may hold values from -1 to 31, as said below
- slot_row: int32 [1024], P(('grp', 'chol')), parts along dimension 0, may hold values from 0 to 31, as said below
Outputs:
- new_walkers: bfloat16 [1024, 64, 256], P(('grp', 'chol')), parts along dimension 0
- force_bias: float32 [1024, 1024], P(('grp', 'chol')), parts along dimension 0
There are 2 independent parts, one for each index of `grp`. A program takes and returns all parts, laid end to end along the dimension named above; an argument that names none is the same for every part. Nothing has to cross between parts.
Inputs may be any that keep to these rules, and one draw needn't show every extreme that they name: `send_walker`: entry [s, d, c] is the index, among the 32 walkers of block s, of the walker that block s sends as its c-th one to block d, or -1 where it sends none; indices of one [s, d] row come first, -1 after. Some pair of blocks uses all 2 entries. `slot_row`: for every slot of block d, s * 2 + c names a valid entry [s, d, c] of send_walker, and every valid entry is named by exactly one slot of block d.
All inputs are finite; a program needn't handle non-finite values.
Results may differ from a plain program's by a relative error of at most 0.0075.
Values may be sent and summed in bfloat16 or wider, within the bound.
A program may use at most 64 MiB of HBM per device.

v0:
```python
import math

import jax
import jax.numpy as jnp
from jax import lax
from jax.sharding import PartitionSpec as P

field_scale = 1.5


def branch_walkers(walkers, send_walker, slot_row):
    slots, electrons, orbitals = walkers.shape
    flat_walkers = walkers.reshape(slots, electrons * orbitals)
    send_list = send_walker.reshape(-1)
    choose_send = (send_list[:, None] == jnp.arange(slots, dtype=jnp.int32)[None, :]).astype(
        jnp.bfloat16
    )
    outgoing = jnp.dot(choose_send, flat_walkers, preferred_element_type=jnp.float32).astype(
        jnp.bfloat16
    )
    incoming = lax.all_to_all(outgoing, "chol", split_axis=0, concat_axis=0, tiled=True)
    choose_recv = (
        slot_row[:, None] == jnp.arange(incoming.shape[0], dtype=jnp.int32)[None, :]
    ).astype(jnp.bfloat16)
    branched = jnp.dot(choose_recv, incoming, preferred_element_type=jnp.float32).astype(
        jnp.bfloat16
    )
    return branched.reshape(slots, electrons, orbitals)


def build_operators(fields, chol_vectors):
    nchol, row_local, orbitals = chol_vectors.shape
    chol_flat = chol_vectors.reshape(nchol, row_local * orbitals)
    scale = field_scale / math.sqrt(nchol)

    def operator_rows(field_rows, first_row):
        return (jnp.dot(field_rows, chol_flat, preferred_element_type=jnp.float32) * scale).astype(
            jnp.bfloat16
        )

    all_rows = operator_rows(lax.all_gather(fields, "chol", axis=0, tiled=True), jnp.int32(0))
    return all_rows.reshape(all_rows.shape[0], row_local, orbitals)


def shards(walkers, fields, chol_vectors, rotated, send_walker, slot_row):
    slots, electrons, orbitals = walkers.shape
    branched = branch_walkers(walkers, send_walker, slot_row)
    operator_rows = build_operators(fields, chol_vectors)
    operator = lax.all_to_all(operator_rows, "chol", split_axis=0, concat_axis=1, tiled=True)
    total = branched.astype(jnp.float32)
    term = branched
    for degree in range(1, 6):
        product = jnp.einsum("waj,wij->wai", term, operator, preferred_element_type=jnp.float32)
        term = (product / degree).astype(jnp.bfloat16)
        total = total + term.astype(jnp.float32)
    new_walkers = total.astype(jnp.bfloat16)
    nchol, elec_local, _ = rotated.shape
    electron_rows = lax.all_to_all(new_walkers, "chol", split_axis=1, concat_axis=0, tiled=True)
    electron_flat = electron_rows.reshape(electron_rows.shape[0], elec_local * orbitals)
    rot_flat = rotated.reshape(nchol, elec_local * orbitals)
    force_bias = lax.psum_scatter(
        lax.dot_general(
            electron_flat, rot_flat, (((1,), (1,)), ((), ())), preferred_element_type=jnp.float32
        ),
        "chol",
        scatter_dimension=0,
        tiled=True,
    )
    return (new_walkers, force_bias)


def solution(mesh):
    in_specs = (
        P(("grp", "chol"), None, None),
        P(("grp", "chol"), None),
        P(None, "chol", None),
        P(None, "chol", None),
        P(("grp", "chol"), None, None),
        P(("grp", "chol")),
    )
    out_specs = (P(("grp", "chol"), None, None), P(("grp", "chol"), None))
    return jax.shard_map(shards, mesh=mesh, in_specs=in_specs, out_specs=out_specs, check_vma=False)
```

profile of v0, /device:TPU:0, one launch (start us, length us, event | category | flops | bytes accessed | tf_op | source)
XLA Modules:
  0.0 282.4 jit_solution(2436412152007579640)
XLA Ops:
  7.2 0.0 copy-start.1
  7.2 0.0 all-gather.2.cloned.1.call-start
  7.2 0.7 all-gather.2.cloned.1.call-update
  7.9 1.8 copy.17
  9.7 0.0 copy-done.1
  9.7 0.1 copy.13
  9.8 0.1 eq.31
  9.9 0.5 convolution_convert_fusion.1
  10.4 1.5 all_to_all.32
  11.9 7.4 %all-to-all-start = ((bf16[16,2,16384]{2,1,0:T(2,128)(2,1)}), bf16[16,2,16384]{2,1,0:T(2,128)(2,1)S(1)}, u32[]{:S(2)}, u32[]{:S(2)}) async-start(bf16[16,2,16384]{2,1,0:T(2,128)(2,1)} %all_to_all.32), calls=%async_computation | async-start | bytes 2097152 | tf_op jit(solution)/shard_map/all_to_all | solution.py:21
  19.3 12.3 %copy.19 = bf16[128,8,16,256]{3,1,2,0:T(8,128)(2,1)} copy(bf16[128,8,16,256]{3,2,1,0:T(8,128)(2,1)} %bitcast.43) | data formatting | bytes 16777216
  31.6 28.7 %all-gather.2.cloned.1.call-done = bf16[512,1024]{1,0:T(8,128)(2,1)} async-done(((bf16[32,1024]{1,0:T(8,128)(2,1)}), bf16[512,1024]{1,0:T(8,128)(2,1)}) %all-gather.2.cloned.1.call-update) | async-done | bytes 1048592 | tf_op jit(solution)/shard_map/all_gather | solution.py:41
  60.3 8.2 %multiply_convert_fusion = bf16[512,4096]{1,0:T(8,128)(2,1)S(1)} fusion(bf16[512,1024]{1,0:T(8,128)(2,1)} %all-gather.2.cloned.1.call-done, bf16[1024,4096]{1,0:T(8,128)(2,1)} %bitcast.44), kind=kOutput, calls=%fused_computation.2 | convolution fusion | flops 4299161600 | bytes 13631488 | tf_op jit(solution)/shard_map/dot_general | solution.py:37
  68.5 3.4 %copy.20 = bf16[64,8,16,256]{3,2,1,0:T(8,128)(2,1)} copy(bf16[64,8,16,256]{3,1,2,0:T(8,128)(2,1)S(1)} %bitcast.47) | data formatting | bytes 8388608
  71.9 0.0 all-to-all-done
  71.9 4.7 %all-to-all-start.1 = ((bf16[512,16,256]{2,1,0:T(8,128)(2,1)}), bf16[512,16,256]{2,1,0:T(8,128)(2,1)}, u32[]{:S(2)}, u32[]{:S(2)}) async-start(bf16[512,16,256]{2,1,0:T(8,128)(2,1)} %bitcast.40), calls=%async_computation.1 | async-start | bytes 8388608 | tf_op jit(solution)/shard_map/all_to_all | solution.py:49
  76.6 0.0 copy-start.2
  76.6 0.4 all_to_all.34
  77.1 0.2 copy-done.2
  77.3 0.5 convolution_convert_fusion
  77.8 0.2 copy.18
  78.0 75.9 %all-to-all-done.1 = bf16[512,16,256]{2,1,0:T(8,128)(2,1)} async-done(((bf16[512,16,256]{2,1,0:T(8,128)(2,1)}), bf16[512,16,256]{2,1,0:T(8,128)(2,1)}, u32[]{:S(2)}, u32[]{:S(2)}) %all-to-all-start.1) | async-done | bytes 4194336 | tf_op jit(solution)/shard_map/all_to_all | solution.py:49
  153.9 2.7 copy.14
  156.7 1.4 convolution_convert_fusion.2
  158.1 1.4 multiply_convert_fusion.4
  159.4 1.4 multiply_convert_fusion.3
  160.8 1.4 multiply_convert_fusion.2
  162.2 1.4 add_convert_fusion
  163.6 0.0 copy-start
  163.6 1.6 copy.15
  165.2 0.0 copy-done
  165.2 19.6 %all-to-all-start.2 = ((bf16[32,64,256]{2,0,1:T(8,128)(2,1)}), bf16[32,64,256]{2,0,1:T(8,128)(2,1)S(1)}, u32[]{:S(2)}, u32[]{:S(2)}) async-start(bf16[32,64,256]{2,0,1:T(8,128)(2,1)} %copy.15), calls=%async_computation.2 | async-start | bytes 2097152 | tf_op jit(solution)/shard_map/all_to_all | solution.py:58
  184.8 0.0 reduce-scatter.2.cloned.1.call-start
  184.8 2.1 copy.22
  186.9 20.8 %all-to-all-done.2 = bf16[32,64,256]{2,0,1:T(8,128)(2,1)S(1)} async-done(((bf16[32,64,256]{2,0,1:T(8,128)(2,1)}), bf16[32,64,256]{2,0,1:T(8,128)(2,1)S(1)}, u32[]{:S(2)}, u32[]{:S(2)}) %all-to-all-start.2) | async-done | bytes 1048608 | tf_op jit(solution)/shard_map/all_to_all | solution.py:58
  207.7 0.9 copy.16
  208.6 0.2 copy.21
  208.8 2.6 fusion.2
  211.4 0.0 reduce-scatter.2.cloned.1.call-update
  211.4 64.1 %reduce-scatter.2.cloned.1.call-done = f32[32,1024]{1,0:T(8,128)} async-done(((f32[512,1024]{1,0:T(8,128)}), f32[32,1024]{1,0:T(8,128)}) %reduce-scatter.2.cloned.1.call-update) | async-done | bytes 131088 | tf_op jit(solution)/shard_map/reduce_scatter | solution.py:61
Async XLA Ops:
  7.2 2.6 copy-start.1
  7.2 53.1 %all-gather.2.cloned.1.call-start = ((), (), s32[]{:S(2)}) async-start(), calls=%async_computation.4 | async-start | bytes 1114112 | tf_op jit(solution)/shard_map/all_gather | solution.py:41
  11.9 60.0 %all-to-all-start = ((bf16[16,2,16384]{2,1,0:T(2,128)(2,1)}), bf16[16,2,16384]{2,1,0:T(2,128)(2,1)S(1)}, u32[]{:S(2)}, u32[]{:S(2)}) async-start(bf16[16,2,16384]{2,1,0:T(2,128)(2,1)} %all_to_all.32), calls=%async_computation | async-start | bytes 2097152 | tf_op jit(solution)/shard_map/all_to_all | solution.py:21
  71.9 82.0 %all-to-all-start.1 = ((bf16[512,16,256]{2,1,0:T(8,128)(2,1)}), bf16[512,16,256]{2,1,0:T(8,128)(2,1)}, u32[]{:S(2)}, u32[]{:S(2)}) async-start(bf16[512,16,256]{2,1,0:T(8,128)(2,1)} %bitcast.40), calls=%async_computation.1 | async-start | bytes 8388608 | tf_op jit(solution)/shard_map/all_to_all | solution.py:49
  76.6 0.7 copy-start.2
  163.6 1.6 copy-start
  165.2 42.5 %all-to-all-start.2 = ((bf16[32,64,256]{2,0,1:T(8,128)(2,1)}), bf16[32,64,256]{2,0,1:T(8,128)(2,1)S(1)}, u32[]{:S(2)}, u32[]{:S(2)}) async-start(bf16[32,64,256]{2,0,1:T(8,128)(2,1)} %copy.15), calls=%async_computation.2 | async-start | bytes 2097152 | tf_op jit(solution)/shard_map/all_to_all | solution.py:58
  184.8 90.7 %reduce-scatter.2.cloned.1.call-start = ((), (), s32[]{:S(2)}) async-start(), calls=%async_computation.5 | async-start | bytes 2228224 | tf_op jit(solution)/shard_map/reduce_scatter | solution.py:61
Sparse Core Ops, SparseCore 0:
  10.1 50.0 all-gather.1
  211.6 63.9 reduce-scatter.1
where the time goes:
time: 283 us; the launch traced here: 282 us
  waiting for transfers between devices  190 us (67%)
  starting transfers between devices  31.8 us (11%)
  local copies, waits for them, and re-layouts  27.5 us (10%)
  matrix products  18.7 us (7%)
  between operations  14.2 us (5%)
    all_to_all x1, waiting for transfers between devices, shards(): lax.all_to_all(operator_rows, 'chol', split_axis=0, concat_axis=1, tiled=...  75.9 us
    reduce_scatter x1, waiting for transfers between devices, shards(): lax.psum_scatter(lax.dot_general(electron_flat, rot_flat, (((1,), (1,)),...  64.1 us
    all_gather x1, waiting for transfers between devices, build_operators(): lax.all_gather(fields, 'chol', axis=0, tiled=True)  28.7 us
    all_to_all x1, waiting for transfers between devices, shards(): lax.all_to_all(new_walkers, 'chol', split_axis=1, concat_axis=0, tiled=True)  20.8 us
    unnamed x13, local copies, waits for them, and re-layouts  20.3 us
    all_to_all x1, starting transfers between devices, shards(): lax.all_to_all(new_walkers, 'chol', split_axis=1, concat_axis=0, tiled=True)  19.6 us
    dot_general x1, matrix products, operator_rows(): jnp.dot(field_rows, chol_flat, preferred_element_type=jnp.float32) * scale  8.22 us
    all_to_all x1, starting transfers between devices, branch_walkers(): lax.all_to_all(outgoing, 'chol', split_axis=0, concat_axis=0, tiled=True)  7.41 us
  transfers between devices with their start and end apart: 5, of which 4 were waited for; matrix products, arithmetic and copies ran while one was open for 10% of the time, Pallas kernels for 0%

commit v1 on v0

v1 whole, which is shorter than its diff:
```python
import functools
import math

import jax
import jax.numpy as jnp
from jax import lax
from jax.experimental import pallas as pl
from jax.experimental.pallas import tpu as pltpu
from jax.sharding import PartitionSpec as P

field_scale = 1.5
chunk_slots = 16
degrees = 5
MESH = pl.DeviceIdType.MESH


def exchange(me, blocks, send, recv, chunk, send_sem, recv_sem):
    def step(k, carry):
        peer = lax.rem(me + k, blocks)
        pltpu.make_async_remote_copy(
            src_ref=send.at[chunk, peer],
            dst_ref=recv.at[chunk, me],
            send_sem=send_sem.at[chunk],
            recv_sem=recv_sem.at[chunk],
            device_id={"chol": peer},
            device_id_type=MESH,
        ).start()
        return carry

    lax.fori_loop(1, blocks, step, 0)
    recv[chunk, me] = send[chunk, me]


def arrived(blocks, recv, chunk, sem):
    whole = recv.at[chunk, pl.ds(0, blocks - 1)]
    pltpu.make_async_copy(whole, whole, sem.at[chunk]).wait()


def kernel(
    dims,
    send_walker,
    slot_row,
    walkers,
    fields,
    chol,
    rotated,
    new_walkers,
    force_bias,
    br_send,
    br_recv,
    op_send,
    op_recv,
    op_rows,
    totals,
    nw_send,
    nw_recv,
    fb_send,
    fb_recv,
    send_sems,
    recv_sems,
):
    blocks, chunks, width, cap, rows, elec = dims
    slots, electrons, orbitals = walkers.shape
    nchol = rotated.shape[0]
    halves = orbitals // 128
    me = lax.axis_index("chol")

    barrier = pltpu.get_barrier_semaphore()

    def greet(k, carry):
        pl.semaphore_signal(
            barrier, inc=1, device_id={"chol": lax.rem(me + k, blocks)}, device_id_type=MESH
        )
        return carry

    lax.fori_loop(1, blocks, greet, 0)

    def pick(d, carry):
        for c in range(cap):
            br_send[0, d, c] = walkers[jnp.maximum(send_walker[d * cap + c], 0)]
        return carry

    lax.fori_loop(0, blocks, pick, 0)
    pl.semaphore_wait(barrier, blocks - 1)
    exchange(me, blocks, br_send, br_recv, 0, send_sems.at[0], recv_sems.at[0])

    scale = field_scale / math.sqrt(nchol)
    cols = rows * orbitals
    tile = min(512, cols)

    @pl.loop(0, cols // tile)
    def _(n):
        at = pl.ds(pl.multiple_of(n * tile, tile), tile)
        part = jnp.dot(fields[...], chol[:, at], preferred_element_type=jnp.float32) * scale
        op_send[:, :, :, at] = part.astype(jnp.bfloat16).reshape(chunks, blocks, width, tile)

    def send_operators(q):
        exchange(me, blocks, op_send, op_recv, q, send_sems.at[1], recv_sems.at[1])

    def taylor(q):
        def spread(s, carry):
            block = op_recv[q, s].astype(jnp.float32)
            for r in range(rows):
                for h in range(halves):
                    low = r * orbitals + h * 128
                    op_rows[h, pl.ds(s * rows + r, width, stride=orbitals), :] = block[
                        :, low : low + 128
                    ]
            return carry

        lax.fori_loop(0, blocks, spread, 0)
        group = 4

        @pl.loop(0, width // group)
        def _(g):
            ops, terms, sums = [], [], []
            for u in range(group):
                w = g * group + u
                first = pl.ds(pl.multiple_of(w * orbitals, orbitals), orbitals)
                ops.append(
                    jnp.concatenate([op_rows[h, first, :] for h in range(halves)], axis=1).astype(
                        jnp.bfloat16
                    )
                )
                row = slot_row[q * width + w]
                terms.append(br_recv[0, row // cap, row % cap])
                sums.append(terms[u].astype(jnp.float32))
            for degree in range(1, degrees + 1):
                for u in range(group):
                    product = lax.dot_general(
                        terms[u],
                        ops[u],
                        (((1,), (1,)), ((), ())),
                        preferred_element_type=jnp.float32,
                    )
                    terms[u] = (product * (1.0 / degree)).astype(jnp.bfloat16)
                    sums[u] = sums[u] + terms[u].astype(jnp.float32)
            for u in range(group):
                w = g * group + u
                new_walkers[q * width + w] = sums[u].astype(jnp.bfloat16)
                place = pl.ds(pl.multiple_of(w * electrons, electrons), electrons)
                for h in range(halves):
                    totals[h, place, :] = sums[u][:, h * 128 : (h + 1) * 128]

        def turn(d, carry):
            for e in range(elec):
                for h in range(halves):
                    low = e * orbitals + h * 128
                    nw_send[q, d, :, low : low + 128] = totals[
                        h, pl.ds(d * elec + e, width, stride=electrons), :
                    ].astype(jnp.bfloat16)
            return carry

        lax.fori_loop(0, blocks, turn, 0)
        exchange(me, blocks, nw_send, nw_recv, q, send_sems.at[2], recv_sems.at[2])

    def bias(q):
        left = nw_recv[q].reshape(blocks * width, elec * orbitals)
        step = min(256, nchol)

        @pl.loop(0, nchol // step)
        def _(n):
            at = pl.ds(pl.multiple_of(n * step, step), step)
            part = lax.dot_general(
                left, rotated[at, :], (((1,), (1,)), ((), ())), preferred_element_type=jnp.float32
            )
            fb_send[q, :, :, at] = part.astype(jnp.bfloat16).reshape(blocks, width, step)

        exchange(me, blocks, fb_send, fb_recv, q, send_sems.at[3], recv_sems.at[3])

    def finish(q):
        force_bias[q * width : (q + 1) * width, :] = lax.fori_loop(
            1,
            blocks,
            lambda s, acc: acc + fb_recv[q, s].astype(jnp.float32),
            fb_recv[q, 0].astype(jnp.float32),
        )

    for q in range(min(2, chunks)):
        send_operators(q)
    arrived(blocks, br_recv, 0, recv_sems.at[0])
    for q in range(chunks + 2):
        if q < chunks:
            arrived(blocks, op_recv, q, recv_sems.at[1])
            if q + 2 < chunks:
                send_operators(q + 2)
            taylor(q)
        if 1 <= q <= chunks:
            arrived(blocks, nw_recv, q - 1, recv_sems.at[2])
            bias(q - 1)
        if q >= 2:
            arrived(blocks, fb_recv, q - 2, recv_sems.at[3])
            finish(q - 2)
    arrived(blocks, br_send, 0, send_sems.at[0])
    for q in range(chunks):
        arrived(blocks, op_send, q, send_sems.at[1])
        arrived(blocks, nw_send, q, send_sems.at[2])
        arrived(blocks, fb_send, q, send_sems.at[3])


def shards(blocks, walkers, fields, chol_vectors, rotated, send_walker, slot_row):
    slots, electrons, orbitals = walkers.shape
    nchol, rows, _ = chol_vectors.shape
    elec = rotated.shape[1]
    cap = send_walker.shape[-1]
    width = min(chunk_slots, slots)
    chunks = slots // width
    gathered = lax.all_gather(fields, "chol", axis=0, tiled=False)
    gathered = gathered.reshape(blocks, chunks, width, nchol).swapaxes(0, 1)
    dims = (blocks, chunks, width, cap, rows, elec)
    bf16, f32 = jnp.bfloat16, jnp.float32
    vmem, smem = (pl.BlockSpec(memory_space=m) for m in (pltpu.VMEM, pltpu.SMEM))
    return pl.pallas_call(
        functools.partial(kernel, dims),
        out_shape=(
            jax.ShapeDtypeStruct(walkers.shape, bf16),
            jax.ShapeDtypeStruct((slots, nchol), f32),
        ),
        in_specs=[smem, smem, vmem, vmem, vmem, vmem],
        out_specs=(vmem, vmem),
        scratch_shapes=[
            pltpu.VMEM((1, blocks, cap, electrons, orbitals), bf16),
            pltpu.VMEM((1, blocks, cap, electrons, orbitals), bf16),
            pltpu.VMEM((chunks, blocks, width, rows * orbitals), bf16),
            pltpu.VMEM((chunks, blocks, width, rows * orbitals), bf16),
            pltpu.VMEM((orbitals // 128, width * orbitals, 128), f32),
            pltpu.VMEM((orbitals // 128, width * electrons, 128), f32),
            pltpu.VMEM((chunks, blocks, width, elec * orbitals), bf16),
            pltpu.VMEM((chunks, blocks, width, elec * orbitals), bf16),
            pltpu.VMEM((chunks, blocks, width, nchol), bf16),
            pltpu.VMEM((chunks, blocks, width, nchol), bf16),
            pltpu.SemaphoreType.DMA((4, chunks)),
            pltpu.SemaphoreType.DMA((4, chunks)),
        ],
        compiler_params=pltpu.CompilerParams(
            collective_id=0, has_side_effects=True, vmem_limit_bytes=60 * 1024 * 1024
        ),
    )(
        send_walker.reshape(-1),
        slot_row,
        walkers,
        gathered.reshape(chunks * blocks * width, nchol),
        chol_vectors.reshape(nchol, rows * orbitals),
        rotated.reshape(nchol, elec * orbitals),
    )


def solution(mesh):
    in_specs = (
        P(("grp", "chol"), None, None),
        P(("grp", "chol"), None),
        P(None, "chol", None),
        P(None, "chol", None),
        P(("grp", "chol"), None, None),
        P(("grp", "chol")),
    )
    out_specs = (P(("grp", "chol"), None, None), P(("grp", "chol"), None))
    return jax.shard_map(
        functools.partial(shards, mesh.shape["chol"]),
        mesh=mesh,
        in_specs=in_specs,
        out_specs=out_specs,
        check_vma=False,
    )
```

time: 283 us -> 231 us (0.82)
  Pallas kernels: 0 us -> 164 us
  waiting for transfers between devices: 190 us -> 26.5 us
  starting transfers between devices: 31.8 us -> 0.04 us
  matrix products: 18.7 us -> 0 us
  local copies, waits for them, and re-layouts: 27.5 us -> 23.2 us
    pallas_call x0 -> x1, Pallas kernels: none -> 164 us  [shards(): pl.pallas_call(functools.partial(kernel, dims), out_shape=(jax.ShapeDtype...]
    all_to_all x3 -> x0, waiting for transfers between devices: 96.7 us -> none  [the longest x1 75.9 us: shards(): lax.all_to_all(operator_rows, 'chol', split_axis=0, concat_axis=1, tiled=...]
    reduce_scatter x1 -> x0, waiting for transfers between devices: 64.1 us -> none  [shards(): lax.psum_scatter(lax.dot_general(electron_flat, rot_flat, (((1,), (1,)),...]
    all_to_all x3 -> x0, starting transfers between devices: 31.8 us -> none  [the longest x1 19.6 us: shards(): lax.all_to_all(new_walkers, 'chol', split_axis=1, concat_axis=0, tiled=True)]
    dot_general x9 -> x0, matrix products: 18.7 us -> none  [the longest x1 8.22 us: operator_rows(): jnp.dot(field_rows, chol_flat, preferred_element_type=jnp.float32) * scale]
    all_to_all x4 -> x0, local copies, waits for them, and re-layouts: 5.56 us -> none  [the longest x1 2.73 us: shards(): lax.all_to_all(operator_rows, 'chol', split_axis=0, concat_axis=1, tiled=...]
    reshape x0 -> x2, local copies, waits for them, and re-layouts: none -> 2.91 us  [the longest x1 2.3 us: shards(): gathered = gathered.reshape(blocks, chunks, width, nchol).swapaxes(0, 1)]
    all_gather x1, waiting for transfers between devices: 28.7 us -> 25.8 us  [shards(): gathered = lax.all_gather(fields, 'chol', axis=0, tiled=False)]
  transfers between devices with their start and end apart: 5 -> 1, of which waited for: 4 -> 1; matrix products, arithmetic and copies ran while one was open for 10% -> 7% of each run, Pallas kernels for 0% -> 0%
where the time goes in v1:
time: 231 us; the launch traced here: 228 us
  Pallas kernels  164 us (71%)
  waiting for transfers between devices  26.5 us (11%)
  local copies, waits for them, and re-layouts  23.2 us (10%)
  between operations  14 us (6%)
    pallas_call x1, Pallas kernels, shards(): pl.pallas_call(functools.partial(kernel, dims), out_shape=(jax.ShapeDtype...  164 us
    all_gather x1, waiting for transfers between devices, shards(): gathered = lax.all_gather(fields, 'chol', axis=0, tiled=False)  25.8 us
    unnamed x5, local copies, waits for them, and re-layouts  20.3 us
  transfers between devices with their start and end apart: 1, of which 1 were waited for; matrix products, arithmetic and copies ran while one was open for 7% of the time, Pallas kernels for 0%

profile of v1, /device:TPU:0, one launch (start us, length us, event | category | flops | bytes accessed | tf_op | source)
XLA Modules:
  0.0 228.0 jit_solution(16557310452246138465)
XLA Ops:
  7.2 0.0 all-gather.3.cloned.1.call-start
  7.2 0.7 all-gather.3.cloned.1.call-update
  7.9 0.8 copy.10
  8.7 0.6 reshape.19.send_walker
  9.3 3.4 %copy.13 = bf16[128,8,4,256]{3,1,2,0:T(8,128)(2,1)} copy(bf16[128,8,4,256]{3,2,1,0:T(4,128)(2,1)} %bitcast.12) | data formatting | bytes 4194304
  12.7 12.2 %copy.12 = bf16[128,8,16,256]{3,1,2,0:T(8,128)(2,1)} copy(bf16[128,8,16,256]{3,2,1,0:T(8,128)(2,1)} %bitcast.10) | data formatting | bytes 16777216
  24.9 25.8 %all-gather.3.cloned.1.call-done = bf16[512,1024]{1,0:T(8,128)(2,1)} async-done(((bf16[32,1024]{1,0:T(8,128)(2,1)}), bf16[512,1024]{1,0:T(8,128)(2,1)}) %all-gather.3.cloned.1.call-update) | async-done | bytes 1048592 | tf_op jit(solution)/shard_map/all_gather | solution.py:208
  50.8 2.3 %copy.11 = bf16[16,2,16,1024]{3,2,0,1:T(8,128)(2,1)} copy(bf16[16,2,16,1024]{3,2,1,0:T(8,128)(2,1)} %bitcast.13) | data formatting | bytes 2097152 | tf_op jit(solution)/shard_map/reshape | solution.py:209
  53.1 164.2 %shard_map.77 = (bf16[32,64,256]{2,1,0:T(8,128)(2,1)}, f32[32,1024]{1,0:T(8,128)}) custom-call(s32[32]{0:T(128)} %reshape.19.send_walker, s32[32]{0:T(128)} %slot_row.1, bf16[32,64,256]{2,1,0:T(8,128)(2,1)} %walkers.1, bf16[512,1024]{1,0:T(8,128)(2,1)} %bitcast.11, bf16[1024,4096]{1,0:T(8,128)(2,1)} %bitcast.8, bf16[1024,1024]{1,0:T(8,128)(2,1)} %bitcast.9), custom_call_target="tpu_custom_call" | custom-call | tf_op jit(solution)/shard_map/pallas_call | solution.py:213
  217.3 2.3 %copy.16 = bf16[32,64,256]{2,1,0:T(8,128)(2,1)} copy(bf16[32,64,256]{2,1,0:T(8,128)(2,1)} %get-tuple-element.4) | data formatting | bytes 2097152
  219.6 1.6 copy.17
Async XLA Ops:
  7.2 43.6 %all-gather.3.cloned.1.call-start = ((), (), s32[]{:S(2)}) async-start(), calls=%async_computation | async-start | bytes 1114112 | tf_op jit(solution)/shard_map/all_gather | solution.py:208
Sparse Core Ops, SparseCore 0:
  10.1 40.5 all-gather.2

commit v2 on v1

--- a/solution.py
+++ b/solution.py
@@ -11,14 +11,35 @@
 field_scale = 1.5
 chunk_slots = 16
 degrees = 5
+unfold_depth = 64
 MESH = pl.DeviceIdType.MESH
 
 
-def exchange(me, blocks, send, recv, chunk, send_sem, recv_sem):
+def unfold(source, scratch, target):
+    depth, rows, orbitals = source.shape
+    step = scratch.shape[1] // rows
+
+    def body(b, carry):
+        first = pl.multiple_of(b * step, step)
+        block = source[pl.ds(first, step)].astype(jnp.float32).reshape(step * rows, orbitals)
+        for h in range(orbitals // 128):
+            scratch[h] = block[:, h * 128 : (h + 1) * 128]
+        for r in range(rows):
+            for h in range(orbitals // 128):
+                low = r * orbitals + h * 128
+                target[pl.ds(first, step), low : low + 128] = scratch[
+                    h, pl.ds(r, step, stride=rows), :
+                ].astype(jnp.bfloat16)
+        return carry
+
+    lax.fori_loop(0, depth // step, body, 0)
+
+
+def exchange(me, blocks, send, recv, chunk, send_sem, recv_sem, place=lambda d: d):
     def step(k, carry):
         peer = lax.rem(me + k, blocks)
         pltpu.make_async_remote_copy(
-            src_ref=send.at[chunk, peer],
+            src_ref=send.at[chunk, place(peer)],
             dst_ref=recv.at[chunk, me],
             send_sem=send_sem.at[chunk],
             recv_sem=recv_sem.at[chunk],
@@ -28,7 +49,7 @@
         return carry
 
     lax.fori_loop(1, blocks, step, 0)
-    recv[chunk, me] = send[chunk, me]
+    recv[chunk, me] = send[chunk, place(me)]
 
 
 def arrived(blocks, recv, chunk, sem):
@@ -42,10 +63,16 @@
     slot_row,
     walkers,
     fields,
-    chol,
-    rotated,
+    chol_hbm,
+    rotated_raw,
     new_walkers,
     force_bias,
+    chol_raw,
+    chol_wide,
+    chol,
+    rotated_wide,
+    rotated,
+    all_fields,
     br_send,
     br_recv,
     op_send,
@@ -58,12 +85,18 @@
     fb_recv,
     send_sems,
     recv_sems,
+    field_sems,
+    load_sem,
 ):
     blocks, chunks, width, cap, rows, elec = dims
     slots, electrons, orbitals = walkers.shape
     nchol = rotated.shape[0]
     halves = orbitals // 128
     me = lax.axis_index("chol")
+    pairs = blocks // 2
+    core, pair = lax.rem(me, 2), me // 2
+    load = pltpu.make_async_copy(chol_hbm, chol_raw, load_sem)
+    load.start()
 
     barrier = pltpu.get_barrier_semaphore()
 
@@ -82,8 +115,36 @@
 
     lax.fori_loop(0, blocks, pick, 0)
     pl.semaphore_wait(barrier, blocks - 1)
+
+    def share(k, carry):
+        pltpu.make_async_remote_copy(
+            src_ref=fields,
+            dst_ref=all_fields.at[core, pair],
+            send_sem=field_sems.at[0],
+            recv_sem=field_sems.at[1],
+            device_id={"chol": lax.rem(pair + k, pairs) * 2 + core},
+            device_id_type=MESH,
+        ).start()
+        return carry
+
+    lax.fori_loop(1, pairs, share, 0)
+    all_fields[core, pair] = fields[...]
+    load.wait()
+    unfold(chol_raw, chol_wide, chol)
+    same_core = all_fields.at[core, pl.ds(0, pairs - 1)]
+    pltpu.make_async_copy(same_core, same_core, field_sems.at[1]).wait()
+    across = pltpu.make_async_remote_copy(
+        src_ref=all_fields.at[core],
+        dst_ref=all_fields.at[core],
+        send_sem=field_sems.at[2],
+        recv_sem=field_sems.at[3],
+        device_id={"chol": pair * 2 + 1 - core},
+        device_id_type=MESH,
+    )
+    across.start()
     exchange(me, blocks, br_send, br_recv, 0, send_sems.at[0], recv_sems.at[0])
 
+    across.wait_recv()
     scale = field_scale / math.sqrt(nchol)
     cols = rows * orbitals
     tile = min(512, cols)
@@ -91,11 +152,17 @@
     @pl.loop(0, cols // tile)
     def _(n):
         at = pl.ds(pl.multiple_of(n * tile, tile), tile)
-        part = jnp.dot(fields[...], chol[:, at], preferred_element_type=jnp.float32) * scale
-        op_send[:, :, :, at] = part.astype(jnp.bfloat16).reshape(chunks, blocks, width, tile)
+        left = all_fields[...].reshape(blocks * slots, nchol)
+        part = jnp.dot(left, chol[:, at], preferred_element_type=jnp.float32) * scale
+        part = part.astype(jnp.bfloat16).reshape(blocks, chunks, width, tile)
+        for q in range(chunks):
+            op_send[q, :, :, at] = part[:, q]
 
     def send_operators(q):
-        exchange(me, blocks, op_send, op_recv, q, send_sems.at[1], recv_sems.at[1])
+        exchange(me, blocks, op_send, op_recv, q, send_sems.at[1], recv_sems.at[1], place)
+
+    def place(d):
+        return lax.rem(d, 2) * pairs + d // 2
 
     def taylor(q):
         def spread(s, carry):
@@ -178,6 +245,7 @@
 
     for q in range(min(2, chunks)):
         send_operators(q)
+    unfold(rotated_raw, rotated_wide, rotated)
     arrived(blocks, br_recv, 0, recv_sems.at[0])
     for q in range(chunks + 2):
         if q < chunks:
@@ -192,6 +260,8 @@
             arrived(blocks, fb_recv, q - 2, recv_sems.at[3])
             finish(q - 2)
     arrived(blocks, br_send, 0, send_sems.at[0])
+    across.wait_send()
+    pltpu.make_async_copy(same_core, same_core, field_sems.at[0]).wait()
     for q in range(chunks):
         arrived(blocks, op_send, q, send_sems.at[1])
         arrived(blocks, nw_send, q, send_sems.at[2])
@@ -205,8 +275,6 @@
     cap = send_walker.shape[-1]
     width = min(chunk_slots, slots)
     chunks = slots // width
-    gathered = lax.all_gather(fields, "chol", axis=0, tiled=False)
-    gathered = gathered.reshape(blocks, chunks, width, nchol).swapaxes(0, 1)
     dims = (blocks, chunks, width, cap, rows, elec)
     bf16, f32 = jnp.bfloat16, jnp.float32
     vmem, smem = (pl.BlockSpec(memory_space=m) for m in (pltpu.VMEM, pltpu.SMEM))
@@ -216,9 +284,15 @@
             jax.ShapeDtypeStruct(walkers.shape, bf16),
             jax.ShapeDtypeStruct((slots, nchol), f32),
         ),
-        in_specs=[smem, smem, vmem, vmem, vmem, vmem],
+        in_specs=[smem, smem, vmem, vmem, pl.BlockSpec(memory_space=pl.ANY), vmem],
         out_specs=(vmem, vmem),
         scratch_shapes=[
+            pltpu.VMEM(chol_vectors.shape, bf16),
+            pltpu.VMEM((orbitals // 128, rows * unfold_depth, 128), f32),
+            pltpu.VMEM((nchol, rows * orbitals), bf16),
+            pltpu.VMEM((orbitals // 128, elec * unfold_depth, 128), f32),
+            pltpu.VMEM((nchol, elec * orbitals), bf16),
+            pltpu.VMEM((2, blocks // 2, slots, nchol), bf16),
             pltpu.VMEM((1, blocks, cap, electrons, orbitals), bf16),
             pltpu.VMEM((1, blocks, cap, electrons, orbitals), bf16),
             pltpu.VMEM((chunks, blocks, width, rows * orbitals), bf16),
@@ -231,6 +305,8 @@
             pltpu.VMEM((chunks, blocks, width, nchol), bf16),
             pltpu.SemaphoreType.DMA((4, chunks)),
             pltpu.SemaphoreType.DMA((4, chunks)),
+            pltpu.SemaphoreType.DMA((4,)),
+            pltpu.SemaphoreType.DMA,
         ],
         compiler_params=pltpu.CompilerParams(
             collective_id=0, has_side_effects=True, vmem_limit_bytes=60 * 1024 * 1024
@@ -239,9 +315,9 @@
         send_walker.reshape(-1),
         slot_row,
         walkers,
-        gathered.reshape(chunks * blocks * width, nchol),
-        chol_vectors.reshape(nchol, rows * orbitals),
-        rotated.reshape(nchol, elec * orbitals),
+        fields,
+        chol_vectors,
+        rotated,
     )
 
 

time: 231 us -> 193 us (0.84)
  waiting for transfers between devices: 26.5 us -> 0 us
  Pallas kernels: 164 us -> 185 us
  local copies, waits for them, and re-layouts: 23.2 us -> 5.23 us
  between operations: 14 us -> 0.64 us
    all_gather x1 -> x0, waiting for transfers between devices: 25.8 us -> none  [shards(): gathered = lax.all_gather(fields, 'chol', axis=0, tiled=False)]
    pallas_call x1, Pallas kernels: 164 us -> 185 us  [shards(): pl.pallas_call(functools.partial(kernel, dims), out_shape=(jax.ShapeDtype...]
    unnamed x5 -> x3, local copies, waits for them, and re-layouts: 20.3 us -> 4.63 us
  transfers between devices with their start and end apart: 1 -> 0, of which waited for: 1 -> 0; matrix products, arithmetic and copies ran while one was open for 7% -> 0% of each run, Pallas kernels for 0% -> 0%
where the time goes in v2:
time: 193 us; the launch traced here: 191 us
  Pallas kernels  185 us (96%)
  local copies, waits for them, and re-layouts  5.23 us (3%)
    pallas_call x1, Pallas kernels, shards(): pl.pallas_call(functools.partial(kernel, dims), out_shape=(jax.ShapeDtype...  185 us
    unnamed x3, local copies, waits for them, and re-layouts  4.63 us

profile of v2, /device:TPU:0, one launch (start us, length us, event | category | flops | bytes accessed | tf_op | source)
XLA Modules:
  0.0 191.2 jit_solution(8362932490009642878)
XLA Ops:
  0.6 0.8 copy.9
  1.4 0.6 reshape.7.send_walker
  2.0 185.3 %shard_map.77 = (bf16[32,64,256]{2,1,0:T(8,128)(2,1)}, f32[32,1024]{1,0:T(8,128)}) custom-call(s32[32]{0:T(128)} %reshape.7.send_walker, s32[32]{0:T(128)} %slot_row.1, bf16[32,64,256]{2,1,0:T(8,128)(2,1)} %walkers.1, bf16[32,1024]{1,0:T(8,128)(2,1)} %fields.1, bf16[1024,16,256]{2,1,0:T(8,128)(2,1)} %chol_hbm.1, bf16[1024,4,256]{2,1,0:T(4,128)(2,1)} %rotated_raw.1), custom_call_target="tpu_custom_call" | custom-call | tf_op jit(solution)/shard_map/pallas_call | solution.py:281
  187.3 2.3 %copy.12 = bf16[32,64,256]{2,1,0:T(8,128)(2,1)} copy(bf16[32,64,256]{2,1,0:T(8,128)(2,1)} %get-tuple-element.4) | data formatting | bytes 2097152
  189.6 1.6 copy.13

commit v3 on v2

--- a/solution.py
+++ b/solution.py
@@ -9,7 +9,7 @@
 from jax.sharding import PartitionSpec as P
 
 field_scale = 1.5
-chunk_slots = 16
+chunk_slots = 8
 degrees = 5
 unfold_depth = 64
 MESH = pl.DeviceIdType.MESH

time: 193 us -> 195 us (1.010)
  Pallas kernels: 185 us -> 189 us
    pallas_call x1, Pallas kernels: 185 us -> 189 us  [shards(): pl.pallas_call(functools.partial(kernel, dims), out_shape=(jax.ShapeDtype...]
where the time goes in v3:
time: 195 us
  Pallas kernels  189 us (97%)
  local copies, waits for them, and re-layouts  5.23 us (3%)
    pallas_call x1, Pallas kernels, shards(): pl.pallas_call(functools.partial(kernel, dims), out_shape=(jax.ShapeDtype...  189 us
    unnamed x3, local copies, waits for them, and re-layouts  4.63 us

profile of v3, /device:TPU:0, one launch (start us, length us, event | category | flops | bytes accessed | tf_op | source)
XLA Modules:
  0.0 194.9 jit_solution(17074166027001496762)
XLA Ops:
  0.6 0.8 copy.9
  1.4 0.6 reshape.7.send_walker
  2.0 189.0 %shard_map.77 = (bf16[32,64,256]{2,1,0:T(8,128)(2,1)}, f32[32,1024]{1,0:T(8,128)}) custom-call(s32[32]{0:T(128)} %reshape.7.send_walker, s32[32]{0:T(128)} %slot_row.1, bf16[32,64,256]{2,1,0:T(8,128)(2,1)} %walkers.1, bf16[32,1024]{1,0:T(8,128)(2,1)} %fields.1, bf16[1024,16,256]{2,1,0:T(8,128)(2,1)} %chol_hbm.1, bf16[1024,4,256]{2,1,0:T(4,128)(2,1)} %rotated_raw.1), custom_call_target="tpu_custom_call" | custom-call | tf_op jit(solution)/shard_map/pallas_call | solution.py:281
  191.0 2.3 %copy.12 = bf16[32,64,256]{2,1,0:T(8,128)(2,1)} copy(bf16[32,64,256]{2,1,0:T(8,128)(2,1)} %get-tuple-element.4) | data formatting | bytes 2097152
  193.3 1.6 copy.13

commit v4 on v2

--- a/solution.py
+++ b/solution.py
@@ -35,12 +35,14 @@
     lax.fori_loop(0, depth // step, body, 0)
 
 
-def exchange(me, blocks, send, recv, chunk, send_sem, recv_sem, place=lambda d: d):
+def exchange(me, blocks, send, recv, chunk, send_sem, recv_sem, place=lambda d: d, land=lambda d: d):
+    hop = next(h for h in (7, 5, 3, 1) if math.gcd(h, blocks) == 1)
+
     def step(k, carry):
-        peer = lax.rem(me + k, blocks)
+        peer = lax.rem(me + k * hop, blocks)
         pltpu.make_async_remote_copy(
             src_ref=send.at[chunk, place(peer)],
-            dst_ref=recv.at[chunk, me],
+            dst_ref=recv.at[chunk, land(me)],
             send_sem=send_sem.at[chunk],
             recv_sem=recv_sem.at[chunk],
             device_id={"chol": peer},
@@ -49,7 +51,7 @@
         return carry
 
     lax.fori_loop(1, blocks, step, 0)
-    recv[chunk, me] = send[chunk, place(me)]
+    recv[chunk, land(me)] = send[chunk, place(me)]
 
 
 def arrived(blocks, recv, chunk, sem):
@@ -81,6 +83,9 @@
     totals,
     nw_send,
     nw_recv,
+    pair_send,
+    pair_recv,
+    pair_own,
     fb_send,
     fb_recv,
     send_sems,
@@ -219,26 +224,54 @@
             return carry
 
         lax.fori_loop(0, blocks, turn, 0)
-        exchange(me, blocks, nw_send, nw_recv, q, send_sems.at[2], recv_sems.at[2])
-
-    def bias(q):
-        left = nw_recv[q].reshape(blocks * width, elec * orbitals)
+        exchange(me, blocks, nw_send, nw_recv, q, send_sems.at[2], recv_sems.at[2], land=place)
+
+    def partial(q, half, target):
+        left = nw_recv[q, pl.ds(half * pairs, pairs)].reshape(pairs * width, elec * orbitals)
         step = min(256, nchol)
 
         @pl.loop(0, nchol // step)
         def _(n):
             at = pl.ds(pl.multiple_of(n * step, step), step)
-            part = lax.dot_general(
+            target[:, at] = lax.dot_general(
                 left, rotated[at, :], (((1,), (1,)), ((), ())), preferred_element_type=jnp.float32
             )
-            fb_send[q, :, :, at] = part.astype(jnp.bfloat16).reshape(blocks, width, step)
-
-        exchange(me, blocks, fb_send, fb_recv, q, send_sems.at[3], recv_sems.at[3])
+
+    def bias(q):
+        partial(q, 1 - core, pair_send.at[q])
+        across = pltpu.make_async_remote_copy(
+            src_ref=pair_send.at[q],
+            dst_ref=pair_recv.at[q],
+            send_sem=send_sems.at[4, q],
+            recv_sem=recv_sems.at[4, q],
+            device_id={"chol": pair * 2 + 1 - core},
+            device_id_type=MESH,
+        )
+        across.start()
+        partial(q, core, pair_own)
+        across.wait_recv()
+        both = (pair_own[...] + pair_recv[q]).astype(jnp.bfloat16)
+        fb_send[q] = both.reshape(pairs, width, nchol)
+
+        def step(k, carry):
+            peer = lax.rem(pair + k, pairs)
+            pltpu.make_async_remote_copy(
+                src_ref=fb_send.at[q, peer],
+                dst_ref=fb_recv.at[q, pair],
+                send_sem=send_sems.at[3, q],
+                recv_sem=recv_sems.at[3, q],
+                device_id={"chol": peer * 2 + core},
+                device_id_type=MESH,
+            ).start()
+            return carry
+
+        lax.fori_loop(1, pairs, step, 0)
+        fb_recv[q, pair] = fb_send[q, pair]
 
     def finish(q):
         force_bias[q * width : (q + 1) * width, :] = lax.fori_loop(
             1,
-            blocks,
+            pairs,
             lambda s, acc: acc + fb_recv[q, s].astype(jnp.float32),
             fb_recv[q, 0].astype(jnp.float32),
         )
@@ -257,7 +290,7 @@
             arrived(blocks, nw_recv, q - 1, recv_sems.at[2])
             bias(q - 1)
         if q >= 2:
-            arrived(blocks, fb_recv, q - 2, recv_sems.at[3])
+            arrived(pairs, fb_recv, q - 2, recv_sems.at[3])
             finish(q - 2)
     arrived(blocks, br_send, 0, send_sems.at[0])
     across.wait_send()
@@ -265,7 +298,8 @@
     for q in range(chunks):
         arrived(blocks, op_send, q, send_sems.at[1])
         arrived(blocks, nw_send, q, send_sems.at[2])
-        arrived(blocks, fb_send, q, send_sems.at[3])
+        arrived(pairs, fb_send, q, send_sems.at[3])
+        pltpu.make_async_copy(pair_send.at[q], pair_send.at[q], send_sems.at[4, q]).wait()
 
 
 def shards(blocks, walkers, fields, chol_vectors, rotated, send_walker, slot_row):
@@ -301,10 +335,13 @@
             pltpu.VMEM((orbitals // 128, width * electrons, 128), f32),
             pltpu.VMEM((chunks, blocks, width, elec * orbitals), bf16),
             pltpu.VMEM((chunks, blocks, width, elec * orbitals), bf16),
-            pltpu.VMEM((chunks, blocks, width, nchol), bf16),
-            pltpu.VMEM((chunks, blocks, width, nchol), bf16),
-            pltpu.SemaphoreType.DMA((4, chunks)),
-            pltpu.SemaphoreType.DMA((4, chunks)),
+            pltpu.VMEM((chunks, blocks // 2 * width, nchol), f32),
+            pltpu.VMEM((chunks, blocks // 2 * width, nchol), f32),
+            pltpu.VMEM((blocks // 2 * width, nchol), f32),
+            pltpu.VMEM((chunks, blocks // 2, width, nchol), bf16),
+            pltpu.VMEM((chunks, blocks // 2, width, nchol), bf16),
+            pltpu.SemaphoreType.DMA((5, chunks)),
+            pltpu.SemaphoreType.DMA((5, chunks)),
             pltpu.SemaphoreType.DMA((4,)),
             pltpu.SemaphoreType.DMA,
         ],

time: 193 us -> 176 us (0.912)
  Pallas kernels: 185 us -> 169 us
    pallas_call x1, Pallas kernels: 185 us -> 169 us  [shards(): pl.pallas_call(functools.partial(kernel, dims), out_shape=(jax.ShapeDtype...]
where the time goes in v4:
time: 176 us; the launch traced here: 175 us
  Pallas kernels  169 us (96%)
  local copies, waits for them, and re-layouts  5.23 us (3%)
    pallas_call x1, Pallas kernels, shards(): pl.pallas_call(functools.partial(kernel, dims), out_shape=(jax.ShapeDtype...  169 us
    unnamed x3, local copies, waits for them, and re-layouts  4.63 us

profile of v4, /device:TPU:0, one launch (start us, length us, event | category | flops | bytes accessed | tf_op | source)
XLA Modules:
  0.0 175.3 jit_solution(2766595633343448077)
XLA Ops:
  0.6 0.8 copy.9
  1.4 0.6 reshape.7.send_walker
  2.0 169.4 %shard_map.77 = (bf16[32,64,256]{2,1,0:T(8,128)(2,1)}, f32[32,1024]{1,0:T(8,128)}) custom-call(s32[32]{0:T(128)} %reshape.7.send_walker, s32[32]{0:T(128)} %slot_row.1, bf16[32,64,256]{2,1,0:T(8,128)(2,1)} %walkers.1, bf16[32,1024]{1,0:T(8,128)(2,1)} %fields.1, bf16[1024,16,256]{2,1,0:T(8,128)(2,1)} %chol_hbm.1, bf16[1024,4,256]{2,1,0:T(4,128)(2,1)} %rotated_raw.1), custom_call_target="tpu_custom_call" | custom-call | tf_op jit(solution)/shard_map/pallas_call | solution.py:315
  171.4 2.3 %copy.12 = bf16[32,64,256]{2,1,0:T(8,128)(2,1)} copy(bf16[32,64,256]{2,1,0:T(8,128)(2,1)} %get-tuple-element.4) | data formatting | bytes 2097152
  173.7 1.6 copy.13

commit v5 on v4

--- a/solution.py
+++ b/solution.py
@@ -13,6 +13,10 @@
 degrees = 5
 unfold_depth = 64
 MESH = pl.DeviceIdType.MESH
+
+
+def stride_of(blocks):
+    return next(h for h in (7, 5, 3, 1) if math.gcd(h, blocks) == 1)
 
 
 def unfold(source, scratch, target):
@@ -36,7 +40,7 @@
 
 
 def exchange(me, blocks, send, recv, chunk, send_sem, recv_sem, place=lambda d: d, land=lambda d: d):
-    hop = next(h for h in (7, 5, 3, 1) if math.gcd(h, blocks) == 1)
+    hop = stride_of(blocks)
 
     def step(k, carry):
         peer = lax.rem(me + k * hop, blocks)
@@ -92,6 +96,7 @@
     recv_sems,
     field_sems,
     load_sem,
+    op_sems,
 ):
     blocks, chunks, width, cap, rows, elec = dims
     slots, electrons, orbitals = walkers.shape
@@ -100,6 +105,9 @@
     me = lax.axis_index("chol")
     pairs = blocks // 2
     core, pair = lax.rem(me, 2), me // 2
+    groups = math.gcd(4, blocks)
+    share_of = blocks // groups
+    hop = stride_of(blocks)
     load = pltpu.make_async_copy(chol_hbm, chol_raw, load_sem)
     load.start()
 
@@ -164,13 +172,28 @@
             op_send[q, :, :, at] = part[:, q]
 
     def send_operators(q):
-        exchange(me, blocks, op_send, op_recv, q, send_sems.at[1], recv_sems.at[1], place)
+        for group in range(groups):
+            def step(k, carry):
+                peer = lax.rem(me + k * hop, blocks)
+                pltpu.make_async_remote_copy(
+                    src_ref=op_send.at[q, place(peer)],
+                    dst_ref=op_recv.at[q, me],
+                    send_sem=send_sems.at[1, q],
+                    recv_sem=op_sems.at[q, group],
+                    device_id={"chol": peer},
+                    device_id_type=MESH,
+                ).start()
+                return carry
+
+            lax.fori_loop(max(1, group * share_of), (group + 1) * share_of, step, 0)
+        op_recv[q, me] = op_send[q, place(me)]
 
     def place(d):
         return lax.rem(d, 2) * pairs + d // 2
 
     def taylor(q):
-        def spread(s, carry):
+        def spread(k, carry):
+            s = lax.rem(me + (blocks - k) * hop, blocks)
             block = op_recv[q, s].astype(jnp.float32)
             for r in range(rows):
                 for h in range(halves):
@@ -180,7 +203,11 @@
                     ]
             return carry
 
-        lax.fori_loop(0, blocks, spread, 0)
+        for group in range(groups):
+            count = share_of - 1 if group == 0 else share_of
+            whole = op_recv.at[q, pl.ds(0, count)]
+            pltpu.make_async_copy(whole, whole, op_sems.at[q, group]).wait()
+            lax.fori_loop(group * share_of, (group + 1) * share_of, spread, 0)
         group = 4
 
         @pl.loop(0, width // group)
@@ -282,7 +309,6 @@
     arrived(blocks, br_recv, 0, recv_sems.at[0])
     for q in range(chunks + 2):
         if q < chunks:
-            arrived(blocks, op_recv, q, recv_sems.at[1])
             if q + 2 < chunks:
                 send_operators(q + 2)
             taylor(q)
@@ -344,6 +370,7 @@
             pltpu.SemaphoreType.DMA((5, chunks)),
             pltpu.SemaphoreType.DMA((4,)),
             pltpu.SemaphoreType.DMA,
+            pltpu.SemaphoreType.DMA((chunks, math.gcd(4, blocks))),
         ],
         compiler_params=pltpu.CompilerParams(
             collective_id=0, has_side_effects=True, vmem_limit_bytes=60 * 1024 * 1024

time: 176 us -> 174 us (0.989)
  no operation moved by 1% of the time
where the time goes in v5:
time: 174 us
  Pallas kernels  168 us (97%)
  local copies, waits for them, and re-layouts  5.23 us (3%)
    pallas_call x1, Pallas kernels, shards(): pl.pallas_call(functools.partial(kernel, dims), out_shape=(jax.ShapeDtype...  168 us
    unnamed x3, local copies, waits for them, and re-layouts  4.63 us

profile of v5, /device:TPU:0, one launch (start us, length us, event | category | flops | bytes accessed | tf_op | source)
XLA Modules:
  0.0 174.1 jit_solution(11486143684339101651)
XLA Ops:
  0.6 0.8 copy.9
  1.4 0.6 reshape.7.send_walker
  2.0 168.3 %shard_map.77 = (bf16[32,64,256]{2,1,0:T(8,128)(2,1)}, f32[32,1024]{1,0:T(8,128)}) custom-call(s32[32]{0:T(128)} %reshape.7.send_walker, s32[32]{0:T(128)} %slot_row.1, bf16[32,64,256]{2,1,0:T(8,128)(2,1)} %walkers.1, bf16[32,1024]{1,0:T(8,128)(2,1)} %fields.1, bf16[1024,16,256]{2,1,0:T(8,128)(2,1)} %chol_hbm.1, bf16[1024,4,256]{2,1,0:T(4,128)(2,1)} %rotated_raw.1), custom_call_target="tpu_custom_call" | custom-call | tf_op jit(solution)/shard_map/pallas_call | solution.py:341
  170.3 2.3 %copy.12 = bf16[32,64,256]{2,1,0:T(8,128)(2,1)} copy(bf16[32,64,256]{2,1,0:T(8,128)(2,1)} %get-tuple-element.4) | data formatting | bytes 2097152
  172.6 1.6 copy.13
